TPU v7x, 256 devices: a whole 4x4x8 slice. The times are simulated.
256 devices in a mesh: seq: 64 (over y, x_hi, z), head: 4 (over x_lo, core).
Axes of the slice: x: 4 (x_hi: 2, x_lo: 2; x = x_hi * 2 + x_lo), y: 4, z: 8, core: 2. Of those that a mesh axis runs over, the one named last changes fastest.
Arguments:
- qkv: bfloat16 [3, 49152, 1536], P(None, ('seq', 'head')), may hold values from -5 to 5
- key_tiles: int32 [12, 128, 27], P('head', 'seq'), may hold values from -1 to 127, as said below
Outputs:
- attended: bfloat16 [49152, 1536], P(('seq', 'head'))
Inputs may be any that keep to these rules, and one draw needn't show every extreme that they name: Each list key_tiles[n, g] names distinct tiles, the query tile g among them, each differing from g by at most 1 in the time tile, the tile row and the tile column; named tiles come first and -1 fills the rest of the list.
All inputs are finite; a program needn't handle non-finite values.
Results may differ from a plain program's by a relative error of at most 0.0035.
Values may be sent and summed in bfloat16 or wider, within the bound.
No kernel may reach another device: no remote copies, remote signals or barrier semaphores. Data moves between devices by JAX's collectives and lax.ppermute only.
A program may use at most 192 MiB of HBM per device.

v0:
```python
import jax
import jax.numpy as jnp
from jax import lax
from jax.sharding import PartitionSpec as P

TIME_TILES = 4
TILE_ROWS = 4


def from_behind(x, axis, by):
    length = lax.axis_size(axis)
    pairs = [(i, i + by) for i in range(length) if 0 <= i + by < length]
    return lax.ppermute(x, axis, pairs)


def swapped(value, axis, distance):
    mask = 2**distance
    pairs = [(source, source ^ mask) for source in range(lax.axis_size(axis))]
    return lax.ppermute(value, axis, pairs)


def attend(query_rows, keys, values, named_mask):
    blocks, slot_count, row_count, head_feature_width = keys.shape
    key_matrix_rows = keys.reshape(blocks, slot_count * row_count, head_feature_width)
    value_matrix_rows = values.reshape(blocks, slot_count * row_count, head_feature_width)
    logit_matrix = jnp.einsum(
        "jxg,jog->jxo", query_rows, key_matrix_rows, preferred_element_type=jnp.float32
    ) * head_feature_width ** (-0.5)
    score_mask = jnp.repeat(named_mask, row_count, axis=1)[:, None, :]
    logit_matrix = jnp.where(score_mask, logit_matrix, -jnp.inf)
    row_max = jnp.max(logit_matrix, axis=-1, keepdims=True)
    weights = jnp.exp(logit_matrix - row_max)
    row_total = jnp.sum(weights, axis=-1, keepdims=True)
    weighted_value_sum = jnp.einsum(
        "aop,ape->aoe",
        weights.astype(jnp.bfloat16),
        value_matrix_rows,
        preferred_element_type=jnp.float32,
    )
    return (weighted_value_sum / row_total).astype(jnp.bfloat16)


def pass_along(block, step_by):
    return from_behind(block, "seq", step_by)


def local(qkv, key_tiles):
    head_count = key_tiles.shape[0]
    col_count = lax.axis_size("seq") * 2 // (TIME_TILES * TILE_ROWS)
    time_stride = 1
    col_stride = 2 * TIME_TILES
    near_cols = 3
    seq_index = lax.axis_index("seq")
    own_time = seq_index % TIME_TILES
    own_pair = seq_index // TIME_TILES % 2
    own_col = seq_index // (2 * TIME_TILES)
    spread = lax.all_to_all(qkv, "head", split_axis=2, concat_axis=1, tiled=True)
    tile_tokens = spread.shape[1] // 2
    head_feature_width = spread.shape[2] // head_count
    query_rows = (
        spread[0].reshape(2, tile_tokens, head_count, head_feature_width).transpose(2, 0, 1, 3)
    )
    kv_pairs = (
        spread[1:3]
        .reshape(2, 2, tile_tokens, head_count, head_feature_width)
        .transpose(0, 3, 1, 2, 4)
    )
    side_bricks = [pass_along(kv_pairs, step_by) for step_by in (col_stride, -col_stride)]
    columns = jnp.stack([side_bricks[0], kv_pairs, side_bricks[1]], axis=2)
    edge_send = jnp.where(own_pair == 0, columns[:, :, :, 1], columns[:, :, :, 0])
    partner_rows = swapped(edge_send, "seq", 2)
    row_stack = jnp.concatenate(
        [partner_rows[:, :, :, None], columns, partner_rows[:, :, :, None]], axis=3
    )
    time_after, time_before = [
        pass_along(row_stack, step_by) for step_by in (-time_stride, time_stride)
    ]
    key_pool = jnp.stack([time_before, row_stack, time_after], axis=2)
    pool_size = 3 * near_cols * 4
    key_flat = key_pool[0].reshape(head_count * pool_size, tile_tokens, head_feature_width)
    value_flat = key_pool[1].reshape(head_count * pool_size, tile_tokens, head_feature_width)
    named_mask = key_tiles >= 0
    safe_tiles = jnp.where(named_mask, key_tiles, 0)
    tile_time = safe_tiles // 2 % TIME_TILES
    tile_row = safe_tiles // (2 * TIME_TILES) % 2 * 2 + safe_tiles % 2
    tile_col = safe_tiles // (4 * TIME_TILES)
    local_index = (
        ((tile_time - own_time + 1) * near_cols + tile_col - own_col + near_cols // 2) * 4
        + tile_row
        - 2 * own_pair
        + 1
    )
    head_base = (jnp.arange(head_count, dtype=jnp.int32) * pool_size)[:, None, None]
    pool_index = jnp.where(named_mask, local_index, 0) + head_base

    def full_block(operands):
        these_queries, these_index, these_named = operands
        return attend(these_queries, key_flat[these_index], value_flat[these_index], these_named)

    attended_tiles = lax.map(full_block, (query_rows, pool_index, named_mask))
    brick_out = attended_tiles.transpose(1, 2, 0, 3).reshape(
        2 * tile_tokens, head_count * head_feature_width
    )
    return lax.all_to_all(brick_out, "head", split_axis=0, concat_axis=1, tiled=True)


def solution(mesh):
    placed = (P(None, ("seq", "head"), None), P("head", "seq", None))
    return jax.shard_map(
        local, mesh=mesh, in_specs=placed, out_specs=P(("seq", "head"), None), check_vma=False
    )
```

profile of v0, /device:TPU:60, one launch (start us, length us, event | category | flops | bytes accessed | tf_op | source)
XLA Modules:
  0.0 656.3 jit_solution(152715509326859987)
XLA Ops:
  5.5 40.6 %all_to_all.34 = bf16[3,192,1536]{1,0,2:T(4,128)(2,1)S(1)} all-to-all(bf16[3,192,1536]{1,0,2:T(4,128)(2,1)} %copy.21), channel_id=1, replica_groups=mesh['seq'=64,'head'=4] {'head'}, dimensions={2} | all-to-all | bytes 3538944 | tf_op jit(solution)/shard_map/all_to_all | solution.py:57
  57.2 22.8 %collective-permute-done.1 = bf16[2,3,2,384,128]{4,3,2,1,0:T(8,128)(2,1)} collective-permute-done((bf16[2,3,2,384,128]{4,3,2,1,0:T(8,128)(2,1)}, bf16[2,3,2,384,128]{4,3,2,1,0:T(8,128)(2,1)}, u32[]{:S(2)}, u32[]{:S(2)}) %collective-permute-start.1) | collective-permute-done | bytes 1179680 | tf_op jit(solution)/shard_map/ppermute | solution.py:13
  82.3 26.7 %collective-permute-done = bf16[2,3,2,384,128]{4,3,2,1,0:T(8,128)(2,1)} collective-permute-done((bf16[2,3,2,384,128]{4,3,2,1,0:T(8,128)(2,1)}, bf16[2,3,2,384,128]{4,3,2,1,0:T(8,128)(2,1)}, u32[]{:S(2)}, u32[]{:S(2)}) %collective-permute-start) | collective-permute-done | bytes 1179680 | tf_op jit(solution)/shard_map/ppermute | solution.py:13
  116.9 6.4 collective-permute-start.2
  123.3 75.6 %collective-permute-done.2 = bf16[2,3,3,384,128]{4,3,2,1,0:T(8,128)(2,1)S(1)} collective-permute-done((bf16[2,3,3,384,128]{4,3,2,1,0:T(8,128)(2,1)S(1)}, bf16[2,3,3,384,128]{4,3,2,1,0:T(8,128)(2,1)S(1)}, u32[]{:S(2)}, u32[]{:S(2)}) %collective-permute-start.2) | collective-permute-done | bytes 1769504 | tf_op jit(solution)/shard_map/ppermute | solution.py:19
  201.9 9.4 %pad_maximum_fusion.1 = bf16[2,3,3,4,384,128]{5,1,4,3,0,2:T(4,128)(2,1)} fusion(bf16[2,3,3,1,384,128]{5,1,4,3,0,2:T(4,128)(2,1)S(1)} %bitcast.96, bf16[2,3,1,2,384,128]{5,1,4,3,0,2:T(4,128)(2,1)S(1)} %bitcast.91, bf16[2,3,1,2,384,128]{5,1,4,3,0,2:T(4,128)(2,1)S(1)} %bitcast.83, bf16[2,3,1,2,384,128]{5,1,4,3,0,2:T(4,128)(2,1)S(1)} %bitcast.94), kind=kLoop, calls=%fused_computation.24 | loop fusion | flops 14155776 | bytes 12386304 | tf_op jit(solution)/shard_map/concatenate | solution.py:72
  211.3 8.5 %copy.29 = bf16[2,3,3,4,384,128]{5,4,3,2,1,0:T(8,128)(2,1)} copy(bf16[2,3,3,4,384,128]{5,1,4,3,0,2:T(4,128)(2,1)} %pad_maximum_fusion.1) | data formatting | bytes 14155776 | tf_op jit(solution)/shard_map/concatenate | solution.py:72
  232.6 10.5 %fusion.37 = bf16[2,3,1,3,4,384,128]{6,1,5,4,0,3,2:T(4,128)(2,1)S(1)} fusion(bf16[2,3,3,1,384,128]{5,1,4,3,0,2:T(4,128)(2,1)} %bitcast.97, bf16[2,3,1,2,384,128]{5,1,4,3,0,2:T(4,128)(2,1)S(1)} %bitcast.92, bf16[2,3,1,2,384,128]{5,1,4,3,0,2:T(4,128)(2,1)S(1)} %bitcast.84, bf16[2,3,1,2,384,128]{5,1,4,3,0,2:T(4,128)(2,1)} %bitcast.95), kind=kLoop, calls=%fused_computation.63 | loop fusion | flops 14155776 | bytes 12386304 | tf_op jit(solution)/shard_map/stack | solution.py:78
  243.2 131.6 %collective-permute-done.4 = bf16[2,3,3,4,384,128]{5,4,3,2,1,0:T(8,128)(2,1)} collective-permute-done((bf16[2,3,3,4,384,128]{5,4,3,2,1,0:T(8,128)(2,1)}, bf16[2,3,3,4,384,128]{5,4,3,2,1,0:T(8,128)(2,1)}, u32[]{:S(2)}, u32[]{:S(2)}) %collective-permute-start.4) | collective-permute-done | bytes 7077920 | tf_op jit(solution)/shard_map/ppermute | solution.py:13
  374.7 10.3 %copy.45 = bf16[2,3,3,4,384,128]{5,1,4,3,0,2:T(4,128)(2,1)S(1)} copy(bf16[2,3,3,4,384,128]{5,4,3,2,1,0:T(8,128)(2,1)} %collective-permute-done.4) | data formatting | bytes 14155776 | tf_op jit(solution)/shard_map/ppermute | solution.py:13
  385.1 11.0 %copy.46 = bf16[2,3,3,4,384,128]{5,1,4,3,0,2:T(4,128)(2,1)} copy(bf16[2,3,3,4,384,128]{5,4,3,2,1,0:T(8,128)(2,1)} %collective-permute-done.3) | data formatting | bytes 14155776 | tf_op jit(solution)/shard_map/ppermute | solution.py:13
  396.1 27.2 %pad_maximum_fusion = bf16[2,3,3,3,4,384,128]{6,1,5,4,0,3,2:T(4,128)(2,1)} fusion(bf16[2,3,1,3,4,384,128]{6,1,5,4,0,3,2:T(4,128)(2,1)S(1)} %bitcast.85, bf16[2,3,1,3,4,384,128]{6,1,5,4,0,3,2:T(4,128)(2,1)S(1)} %fusion.37, bf16[2,3,1,3,4,384,128]{6,1,5,4,0,3,2:T(4,128)(2,1)} %bitcast.86), kind=kLoop, calls=%fused_computation.23 | loop fusion | flops 21233664 | bytes 42467328 | tf_op jit(solution)/shard_map/stack | solution.py:78
  423.3 19.9 %fusion.34 = (bf16[1,3,3,3,4,384,128]{6,1,5,4,0,3,2:T(4,128)(2,1)}, bf16[1,3,3,3,4,384,128]{6,1,5,4,0,3,2:T(4,128)(2,1)}) fusion(bf16[2,3,3,3,4,384,128]{6,1,5,4,0,3,2:T(4,128)(2,1)} %pad_maximum_fusion), kind=kLoop, calls=%fused_computation.62 | loop fusion | bytes 42467328 | tf_op jit(solution)/shard_map/slice | solution.py:81
  443.2 12.1 %copy.33 = bf16[1,3,3,3,4,384,128]{6,5,4,3,2,1,0:T(8,128)(2,1)} copy(bf16[1,3,3,3,4,384,128]{6,1,5,4,0,3,2:T(4,128)(2,1)} %get-tuple-element.81) | data formatting | bytes 21233664 | tf_op jit(solution)/shard_map/slice | solution.py:80
  456.3 5.7 copy.34
  462.0 180.4 %while.10 = (s32[]{:T(128)}, bf16[3,2,384,128]{3,2,1,0:T(8,128)(2,1)S(1)}, pred[3,2,27]{2,1,0:T(4,128)(4,1)S(1)}, bf16[3,2,384,128]{3,2,1,0:T(8,128)(2,1)}, s32[...) while((s32[]{:T(128)}, ...), condition=%wide.region_3.4_spmd, body=%wide.region_0.3_spmd.sunk | while | flops 4164648448 | bytes 127962088 | solution.py:100
  462.1 7.7 %gather_fusion.1 = bf16[54,384,128]{2,1,0:T(8,128)(2,1)} fusion(bf16[108,384,128]{2,1,0:T(8,128)(2,1)} %get-tuple-element.150, s32[1024]{0:T(1024)S(1)} %pad_clamp_fusion.2), kind=kCustom, calls=%fused_computation.clone.1 | custom fusion | bytes 10617048 | tf_op jit(solution)/shard_map/while/body/eval_jaxpr/gather | solution.py:98
  469.9 14.9 %fusion.47 = (f32[2,384]{1,0:T(2,128)S(1)}, f32[2,384,10368]{2,1,0:T(8,128)}) fusion(pred[2,10368]{1,0:T(4,128)(4,1)S(1)} %bitcast.87, bf16[2,10368,128]{2,1,0:T(8,128)(2,1)} %bitcast.77, bf16[3,2,384,128]{3,2,1,0:T(8,128)(2,1)} %get-tuple-element.148, s32[]{:T(128)} %get-tuple-element.137), kind=kOutput, calls=%fused_computation.4.clone.1 | convolution fusion | flops 2062318848 | bytes 37379840 | tf_op jit(solution)/shard_map/while/body/eval_jaxpr/jxg,jog->jxo/dot_general | solution.py:26
  484.7 14.3 %fusion.48 = f32[2,384]{1,0:T(2,128)S(1)} fusion(f32[2,384,10368]{2,1,0:T(8,128)} %get-tuple-element.127, f32[2,384]{1,0:T(2,128)S(1)} %get-tuple-element.128, pred[2,10368]{1,0:T(4,128)(4,1)S(1)} %bitcast.88), kind=kLoop, calls=%fused_computation.5.clone.1 | loop fusion | flops 31849728 | bytes 31877376 | tf_op jit(solution)/shard_map/while/body/eval_jaxpr/reduce_sum | solution.py:33
  499.0 7.7 %gather_fusion = bf16[54,384,128]{2,1,0:T(8,128)(2,1)} fusion(bf16[108,384,128]{2,1,0:T(8,128)(2,1)} %get-tuple-element.151, s32[1024]{0:T(1024)S(1)} %pad_clamp_fusion.2), kind=kCustom, calls=%fused_computation.1.clone.1 | custom fusion | bytes 10617048 | tf_op jit(solution)/shard_map/while/body/eval_jaxpr/gather | solution.py:98
  506.7 15.4 %fusion.49 = bf16[3,2,384,128]{3,2,1,0:T(8,128)(2,1)S(1)} fusion(bf16[3,2,384,128]{3,2,1,0:T(8,128)(2,1)S(1)} %get-tuple-element.138, s32[]{:T(128)} %get-tuple-element.137, bf16[2,10368,128]{2,1,0:T(8,128)(2,1)} %bitcast.78, f32[2,384,10368]{2,1,0:T(8,128)} %get-tuple-element.127, f32[2,384]{1,0:T(2,128)S(1)} %get-tuple-element.128, ...), kind=kOutput, calls=%fused_computation.12.clone.1 | convolution fusion | flops 2070478848 | bytes 37403140 | tf_op jit(solution)/shard_map/while/body/eval_jaxpr/aop,ape->aoe/dot_general | solution.py:34
  522.2 7.7 %gather_fusion.1 = bf16[54,384,128]{2,1,0:T(8,128)(2,1)} fusion(bf16[108,384,128]{2,1,0:T(8,128)(2,1)} %get-tuple-element.150, s32[1024]{0:T(1024)S(1)} %pad_clamp_fusion.2), kind=kCustom, calls=%fused_computation.clone.1 | custom fusion | bytes 10617048 | tf_op jit(solution)/shard_map/while/body/eval_jaxpr/gather | solution.py:98
  530.0 14.9 %fusion.47 = (f32[2,384]{1,0:T(2,128)S(1)}, f32[2,384,10368]{2,1,0:T(8,128)}) fusion(pred[2,10368]{1,0:T(4,128)(4,1)S(1)} %bitcast.87, bf16[2,10368,128]{2,1,0:T(8,128)(2,1)} %bitcast.77, bf16[3,2,384,128]{3,2,1,0:T(8,128)(2,1)} %get-tuple-element.148, s32[]{:T(128)} %get-tuple-element.137), kind=kOutput, calls=%fused_computation.4.clone.1 | convolution fusion | flops 2062318848 | bytes 37379840 | tf_op jit(solution)/shard_map/while/body/eval_jaxpr/jxg,jog->jxo/dot_general | solution.py:26
  544.9 14.3 %fusion.48 = f32[2,384]{1,0:T(2,128)S(1)} fusion(f32[2,384,10368]{2,1,0:T(8,128)} %get-tuple-element.127, f32[2,384]{1,0:T(2,128)S(1)} %get-tuple-element.128, pred[2,10368]{1,0:T(4,128)(4,1)S(1)} %bitcast.88), kind=kLoop, calls=%fused_computation.5.clone.1 | loop fusion | flops 31849728 | bytes 31877376 | tf_op jit(solution)/shard_map/while/body/eval_jaxpr/reduce_sum | solution.py:33
  559.2 7.7 %gather_fusion = bf16[54,384,128]{2,1,0:T(8,128)(2,1)} fusion(bf16[108,384,128]{2,1,0:T(8,128)(2,1)} %get-tuple-element.151, s32[1024]{0:T(1024)S(1)} %pad_clamp_fusion.2), kind=kCustom, calls=%fused_computation.1.clone.1 | custom fusion | bytes 10617048 | tf_op jit(solution)/shard_map/while/body/eval_jaxpr/gather | solution.py:98
  566.8 15.4 %fusion.49 = bf16[3,2,384,128]{3,2,1,0:T(8,128)(2,1)S(1)} fusion(bf16[3,2,384,128]{3,2,1,0:T(8,128)(2,1)S(1)} %get-tuple-element.138, s32[]{:T(128)} %get-tuple-element.137, bf16[2,10368,128]{2,1,0:T(8,128)(2,1)} %bitcast.78, f32[2,384,10368]{2,1,0:T(8,128)} %get-tuple-element.127, f32[2,384]{1,0:T(2,128)S(1)} %get-tuple-element.128, ...), kind=kOutput, calls=%fused_computation.12.clone.1 | convolution fusion | flops 2070478848 | bytes 37403140 | tf_op jit(solution)/shard_map/while/body/eval_jaxpr/aop,ape->aoe/dot_general | solution.py:34
  582.4 7.7 %gather_fusion.1 = bf16[54,384,128]{2,1,0:T(8,128)(2,1)} fusion(bf16[108,384,128]{2,1,0:T(8,128)(2,1)} %get-tuple-element.150, s32[1024]{0:T(1024)S(1)} %pad_clamp_fusion.2), kind=kCustom, calls=%fused_computation.clone.1 | custom fusion | bytes 10617048 | tf_op jit(solution)/shard_map/while/body/eval_jaxpr/gather | solution.py:98
  590.2 14.9 %fusion.47 = (f32[2,384]{1,0:T(2,128)S(1)}, f32[2,384,10368]{2,1,0:T(8,128)}) fusion(pred[2,10368]{1,0:T(4,128)(4,1)S(1)} %bitcast.87, bf16[2,10368,128]{2,1,0:T(8,128)(2,1)} %bitcast.77, bf16[3,2,384,128]{3,2,1,0:T(8,128)(2,1)} %get-tuple-element.148, s32[]{:T(128)} %get-tuple-element.137), kind=kOutput, calls=%fused_computation.4.clone.1 | convolution fusion | flops 2062318848 | bytes 37379840 | tf_op jit(solution)/shard_map/while/body/eval_jaxpr/jxg,jog->jxo/dot_general | solution.py:26
  605.0 14.3 %fusion.48 = f32[2,384]{1,0:T(2,128)S(1)} fusion(f32[2,384,10368]{2,1,0:T(8,128)} %get-tuple-element.127, f32[2,384]{1,0:T(2,128)S(1)} %get-tuple-element.128, pred[2,10368]{1,0:T(4,128)(4,1)S(1)} %bitcast.88), kind=kLoop, calls=%fused_computation.5.clone.1 | loop fusion | flops 31849728 | bytes 31877376 | tf_op jit(solution)/shard_map/while/body/eval_jaxpr/reduce_sum | solution.py:33
  619.3 7.7 %gather_fusion = bf16[54,384,128]{2,1,0:T(8,128)(2,1)} fusion(bf16[108,384,128]{2,1,0:T(8,128)(2,1)} %get-tuple-element.151, s32[1024]{0:T(1024)S(1)} %pad_clamp_fusion.2), kind=kCustom, calls=%fused_computation.1.clone.1 | custom fusion | bytes 10617048 | tf_op jit(solution)/shard_map/while/body/eval_jaxpr/gather | solution.py:98
  627.0 15.4 %fusion.49 = bf16[3,2,384,128]{3,2,1,0:T(8,128)(2,1)S(1)} fusion(bf16[3,2,384,128]{3,2,1,0:T(8,128)(2,1)S(1)} %get-tuple-element.138, s32[]{:T(128)} %get-tuple-element.137, bf16[2,10368,128]{2,1,0:T(8,128)(2,1)} %bitcast.78, f32[2,384,10368]{2,1,0:T(8,128)} %get-tuple-element.127, f32[2,384]{1,0:T(2,128)S(1)} %get-tuple-element.128, ...), kind=kOutput, calls=%fused_computation.12.clone.1 | convolution fusion | flops 2070478848 | bytes 37403140 | tf_op jit(solution)/shard_map/while/body/eval_jaxpr/aop,ape->aoe/dot_general | solution.py:34
  643.5 11.9 %all_to_all.35 = bf16[4,192,384]{2,1,0:T(8,128)(2,1)S(1)} all-to-all(bf16[4,192,384]{2,1,0:T(8,128)(2,1)S(1)} %all_to_all.28), channel_id=1, replica_groups=mesh['seq'=64,'head'=4] {'head'}, dimensions={0} | all-to-all | bytes 1179648 | tf_op jit(solution)/shard_map/all_to_all | solution.py:104
  (54 shorter events, 46.0 us)
Async XLA Ops:
  52.5 27.6 %collective-permute-start.1 = (bf16[2,3,2,384,128]{4,3,2,1,0:T(8,128)(2,1)}, bf16[2,3,2,384,128]{4,3,2,1,0:T(8,128)(2,1)}, u32[]{:S(2)}, u32[]{:S(2)}) collective-permute-start(bf16[2,3,2,384,128]{4,3,2,1,0:T(8,128)(2,1)} %copy.23), channel_id=1, source_target_pairs={{32,0},{36,4},{40,8},{44,12},{48,16},{52,20},{56,24},{60,28},{64,3... | collective-permute-start | bytes 3538952 | tf_op jit(solution)/shard_map/ppermute | solution.py:13
  55.9 53.1 %collective-permute-start = (bf16[2,3,2,384,128]{4,3,2,1,0:T(8,128)(2,1)}, bf16[2,3,2,384,128]{4,3,2,1,0:T(8,128)(2,1)}, u32[]{:S(2)}, u32[]{:S(2)}) collective-permute-start(bf16[2,3,2,384,128]{4,3,2,1,0:T(8,128)(2,1)} %copy.23), channel_id=1, source_target_pairs={{0,32},{4,36},{8,40},{12,44},{16,48},{20,52},{24,56},{28,60},{32,6... | collective-permute-start | bytes 3538952 | tf_op jit(solution)/shard_map/ppermute | solution.py:13
  111.3 89.2 %copy-start.1 = (bf16[2,3,2,384,128]{4,1,3,2,0:T(4,128)(2,1)}, bf16[2,3,2,384,128]{4,1,3,2,0:T(4,128)(2,1)S(1)}, u32[]{:S(2)}) copy-start(bf16[2,3,2,384,128]{4,1,3,2,0:T(4,128)(2,1)S(1)} %copy.49) | copy-start | bytes 3538948
  116.9 82.0 %collective-permute-start.2 = (bf16[2,3,3,384,128]{4,3,2,1,0:T(8,128)(2,1)S(1)}, bf16[2,3,3,384,128]{4,3,2,1,0:T(8,128)(2,1)S(1)}, u32[]{:S(2)}, u32[]{:S(2)}) collective-permute-start(bf16[2,3,3,384,128]{4,3,2,1,0:T(8,128)(2,1)S(1)} %copy.27), channel_id=1, source_target_pairs={{0,16},{4,20},{8,24},{12,28},{16,0},{20,4},{24,8},{28,12},{32,48},... | collective-permute-start | bytes 5308424 | tf_op jit(solution)/shard_map/ppermute | solution.py:19
  200.5 1.5 copy-start.2
  211.3 14.6 %copy-start.4 = (s32[3,2,27]{2,1,0:T(2,128)S(1)}, s32[3,2,27]{2,1,0:T(2,128)}, u32[]{:S(2)}) copy-start(s32[3,2,27]{2,1,0:T(2,128)} %param.5) | copy-start | bytes 1948
  219.8 154.9 %collective-permute-start.4 = (bf16[2,3,3,4,384,128]{5,4,3,2,1,0:T(8,128)(2,1)}, bf16[2,3,3,4,384,128]{5,4,3,2,1,0:T(8,128)(2,1)}, u32[]{:S(2)}, u32[]{:S(2)}) collective-permute-start(bf16[2,3,3,4,384,128]{5,4,3,2,1,0:T(8,128)(2,1)} %copy.29), channel_id=1, source_target_pairs={{4,0},{8,4},{12,8},{16,12},{20,16},{24,20},{28,24},{32,28},{36,32}... | collective-permute-start | bytes 21233672 | tf_op jit(solution)/shard_map/ppermute | solution.py:13
  221.7 163.3 %collective-permute-start.3 = (bf16[2,3,3,4,384,128]{5,4,3,2,1,0:T(8,128)(2,1)}, bf16[2,3,3,4,384,128]{5,4,3,2,1,0:T(8,128)(2,1)}, u32[]{:S(2)}, u32[]{:S(2)}) collective-permute-start(bf16[2,3,3,4,384,128]{5,4,3,2,1,0:T(8,128)(2,1)} %copy.29), channel_id=1, source_target_pairs={{0,4},{4,8},{8,12},{12,16},{16,20},{20,24},{24,28},{28,32},{32,36}... | collective-permute-start | bytes 21233672 | tf_op jit(solution)/shard_map/ppermute | solution.py:13
  443.2 13.1 %copy-start = (bf16[1,3,3,3,4,384,128]{6,1,5,4,0,3,2:T(4,128)(2,1)S(1)}, bf16[1,3,3,3,4,384,128]{6,1,5,4,0,3,2:T(4,128)(2,1)}, u32[]{:S(2)}) copy-start(bf16[1,3,3,3,4,384,128]{6,1,5,4,0,3,2:T(4,128)(2,1)} %get-tuple-element.80) | copy-start | bytes 31850500
  456.3 5.7 copy-start.3
where the time goes:
time: 658 us; the launch traced here: 656 us
  waiting for transfers between devices  257 us (39%)
  local copies, waits for them, and re-layouts  143 us (22%)
  other arithmetic  95.3 us (14%)
  matrix products  90.9 us (14%)
  blocking collectives  52.5 us (8%)
  starting transfers between devices  17.1 us (3%)
    ppermute x4, waiting for transfers between devices, from_behind(): return lax.ppermute(x, axis, pairs)  181 us
    ppermute x1, waiting for transfers between devices, swapped(): return lax.ppermute(value, axis, pairs)  75.6 us
    dot_general x3, matrix products, attend(): jnp.einsum('aop,ape->aoe', weights.astype(jnp.bfloat16), value_matrix_row...  46.3 us
    dot_general x3, matrix products, attend(): jnp.einsum('jxg,jog->jxo', query_rows, key_matrix_rows, preferred_element...  44.6 us
    reduce_sum x3, other arithmetic, attend(): row_total = jnp.sum(weights, axis=-1, keepdims=True)  42.8 us
    all_to_all x1, blocking collectives, local(): lax.all_to_all(qkv, 'head', split_axis=2, concat_axis=1, tiled=True)  40.6 us
    another operation x2, other arithmetic, local(): key_pool = jnp.stack([time_before, row_stack, time_after], axis=2)  37.7 us
    ppermute x4, local copies, waits for them, and re-layouts, from_behind(): return lax.ppermute(x, axis, pairs)  25.9 us
  transfers between devices with their start and end apart: 5, of which 4 were waited for; matrix products, arithmetic and copies ran while one was open for 5% of the time, Pallas kernels for 0%

commit v1 on v0

--- a/solution.py
+++ b/solution.py
@@ -54,7 +54,10 @@
     own_time = seq_index % TIME_TILES
     own_pair = seq_index // TIME_TILES % 2
     own_col = seq_index // (2 * TIME_TILES)
-    spread = lax.all_to_all(qkv, "head", split_axis=2, concat_axis=1, tiled=True)
+    spread = jnp.concatenate(
+        lax.all_to_all(jnp.stack(jnp.split(qkv, lax.axis_size("head"), axis=2)), "head", 0, 0),
+        axis=1,
+    )
     tile_tokens = spread.shape[1] // 2
     head_feature_width = spread.shape[2] // head_count
     query_rows = (

time: 658 us -> 635 us (0.965)
  blocking collectives: 52.5 us -> 36.6 us
  local copies, waits for them, and re-layouts: 143 us -> 136 us
    all_to_all x1, blocking collectives: 40.6 us -> 24.6 us  [local(): lax.all_to_all(jnp.stack(jnp.split(qkv, lax.axis_size('head'), axis=2)),...]
where the time goes in v1:
time: 635 us; the launch traced here: 634 us
  waiting for transfers between devices  257 us (40%)
  local copies, waits for them, and re-layouts  136 us (21%)
  other arithmetic  95.6 us (15%)
  matrix products  90.7 us (14%)
  blocking collectives  36.6 us (6%)
  starting transfers between devices  17.2 us (3%)
    ppermute x4, waiting for transfers between devices, from_behind(): return lax.ppermute(x, axis, pairs)  181 us
    ppermute x1, waiting for transfers between devices, swapped(): return lax.ppermute(value, axis, pairs)  76 us
    dot_general x3, matrix products, attend(): jnp.einsum('aop,ape->aoe', weights.astype(jnp.bfloat16), value_matrix_row...  46.3 us
    dot_general x3, matrix products, attend(): jnp.einsum('jxg,jog->jxo', query_rows, key_matrix_rows, preferred_element...  44.4 us
    reduce_sum x3, other arithmetic, attend(): row_total = jnp.sum(weights, axis=-1, keepdims=True)  42.8 us
    another operation x2, other arithmetic, local(): key_pool = jnp.stack([time_before, row_stack, time_after], axis=2)  37.8 us
    ppermute x4, local copies, waits for them, and re-layouts, from_behind(): return lax.ppermute(x, axis, pairs)  25.9 us
    slice x2, local copies, waits for them, and re-layouts, local(): key_pool[1].reshape(head_count * pool_size, tile_tokens, head_feature_width)  25.7 us
  transfers between devices with their start and end apart: 5, of which 4 were waited for; matrix products, arithmetic and copies ran while one was open for 5% of the time, Pallas kernels for 0%

profile of v1, /device:TPU:60, one launch (start us, length us, event | category | flops | bytes accessed | tf_op | source)
XLA Modules:
  0.0 634.0 jit_solution(10203485765463250554)
XLA Ops:
  1.9 24.6 %all_to_all.24 = bf16[4,3,192,384]{3,2,1,0:T(8,128)(2,1)S(1)} all-to-all(bf16[4,3,192,384]{3,2,1,0:T(8,128)(2,1)S(1)} %pad_maximum_fusion.3), channel_id=1, replica_groups=mesh['seq'=64,'head'=4] {'head'}, dimensions={0} | all-to-all | bytes 3538944 | tf_op jit(solution)/shard_map/all_to_all | solution.py:58
  34.4 23.1 %collective-permute-done.1 = bf16[2,3,2,384,128]{4,3,2,1,0:T(8,128)(2,1)} collective-permute-done((bf16[2,3,2,384,128]{4,3,2,1,0:T(8,128)(2,1)}, bf16[2,3,2,384,128]{4,3,2,1,0:T(8,128)(2,1)}, u32[]{:S(2)}, u32[]{:S(2)}) %collective-permute-start.1) | collective-permute-done | bytes 1179680 | tf_op jit(solution)/shard_map/ppermute | solution.py:13
  59.8 26.5 %collective-permute-done = bf16[2,3,2,384,128]{4,3,2,1,0:T(8,128)(2,1)} collective-permute-done((bf16[2,3,2,384,128]{4,3,2,1,0:T(8,128)(2,1)}, bf16[2,3,2,384,128]{4,3,2,1,0:T(8,128)(2,1)}, u32[]{:S(2)}, u32[]{:S(2)}) %collective-permute-start) | collective-permute-done | bytes 1179680 | tf_op jit(solution)/shard_map/ppermute | solution.py:13
  94.2 6.4 %collective-permute-start.2 = (bf16[2,3,3,384,128]{4,3,2,1,0:T(8,128)(2,1)S(1)}, bf16[2,3,3,384,128]{4,3,2,1,0:T(8,128)(2,1)S(1)}, u32[]{:S(2)}, u32[]{:S(2)}) collective-permute-start(bf16[2,3,3,384,128]{4,3,2,1,0:T(8,128)(2,1)S(1)} %copy.26), channel_id=1, source_target_pairs={{0,16},{4,20},{8,24},{12,28},{16,0},{20,4},{24,8},{28,12},{32,48},... | collective-permute-start | bytes 5308424 | tf_op jit(solution)/shard_map/ppermute | solution.py:19
  100.6 76.0 %collective-permute-done.2 = bf16[2,3,3,384,128]{4,3,2,1,0:T(8,128)(2,1)S(1)} collective-permute-done((bf16[2,3,3,384,128]{4,3,2,1,0:T(8,128)(2,1)S(1)}, bf16[2,3,3,384,128]{4,3,2,1,0:T(8,128)(2,1)S(1)}, u32[]{:S(2)}, u32[]{:S(2)}) %collective-permute-start.2) | collective-permute-done | bytes 1769504 | tf_op jit(solution)/shard_map/ppermute | solution.py:19
  179.6 9.4 %pad_maximum_fusion.1 = bf16[2,3,3,4,384,128]{5,1,4,3,0,2:T(4,128)(2,1)} fusion(bf16[2,3,3,1,384,128]{5,1,4,3,0,2:T(4,128)(2,1)S(1)} %bitcast.105, bf16[2,3,1,2,384,128]{5,1,4,3,0,2:T(4,128)(2,1)S(1)} %bitcast.100, bf16[2,3,1,2,384,128]{5,1,4,3,0,2:T(4,128)(2,1)S(1)} %bitcast.92, bf16[2,3,1,2,384,128]{5,1,4,3,0,2:T(4,128)(2,1)S(1)} %bitcast.103), kind=kLoop, calls=%fused_computation.24 | loop fusion | flops 14155776 | bytes 12386304 | tf_op jit(solution)/shard_map/concatenate | solution.py:75
  189.0 8.5 %copy.28 = bf16[2,3,3,4,384,128]{5,4,3,2,1,0:T(8,128)(2,1)} copy(bf16[2,3,3,4,384,128]{5,1,4,3,0,2:T(4,128)(2,1)} %pad_maximum_fusion.1) | data formatting | bytes 14155776 | tf_op jit(solution)/shard_map/concatenate | solution.py:75
  210.3 10.5 %fusion.37 = bf16[2,3,1,3,4,384,128]{6,1,5,4,0,3,2:T(4,128)(2,1)S(1)} fusion(bf16[2,3,3,1,384,128]{5,1,4,3,0,2:T(4,128)(2,1)} %bitcast.106, bf16[2,3,1,2,384,128]{5,1,4,3,0,2:T(4,128)(2,1)S(1)} %bitcast.101, bf16[2,3,1,2,384,128]{5,1,4,3,0,2:T(4,128)(2,1)S(1)} %bitcast.93, bf16[2,3,1,2,384,128]{5,1,4,3,0,2:T(4,128)(2,1)} %bitcast.104), kind=kLoop, calls=%fused_computation.68 | loop fusion | flops 14155776 | bytes 12386304 | tf_op jit(solution)/shard_map/stack | solution.py:81
  220.8 131.6 %collective-permute-done.4 = bf16[2,3,3,4,384,128]{5,4,3,2,1,0:T(8,128)(2,1)} collective-permute-done((bf16[2,3,3,4,384,128]{5,4,3,2,1,0:T(8,128)(2,1)}, bf16[2,3,3,4,384,128]{5,4,3,2,1,0:T(8,128)(2,1)}, u32[]{:S(2)}, u32[]{:S(2)}) %collective-permute-start.4) | collective-permute-done | bytes 7077920 | tf_op jit(solution)/shard_map/ppermute | solution.py:13
  352.4 10.3 %copy.44 = bf16[2,3,3,4,384,128]{5,1,4,3,0,2:T(4,128)(2,1)S(1)} copy(bf16[2,3,3,4,384,128]{5,4,3,2,1,0:T(8,128)(2,1)} %collective-permute-done.4) | data formatting | bytes 14155776 | tf_op jit(solution)/shard_map/ppermute | solution.py:13
  362.7 11.1 %copy.45 = bf16[2,3,3,4,384,128]{5,1,4,3,0,2:T(4,128)(2,1)} copy(bf16[2,3,3,4,384,128]{5,4,3,2,1,0:T(8,128)(2,1)} %collective-permute-done.3) | data formatting | bytes 14155776 | tf_op jit(solution)/shard_map/ppermute | solution.py:13
  373.8 27.2 %pad_maximum_fusion = bf16[2,3,3,3,4,384,128]{6,1,5,4,0,3,2:T(4,128)(2,1)} fusion(bf16[2,3,1,3,4,384,128]{6,1,5,4,0,3,2:T(4,128)(2,1)S(1)} %bitcast.94, bf16[2,3,1,3,4,384,128]{6,1,5,4,0,3,2:T(4,128)(2,1)S(1)} %fusion.37, bf16[2,3,1,3,4,384,128]{6,1,5,4,0,3,2:T(4,128)(2,1)} %bitcast.95), kind=kLoop, calls=%fused_computation.23 | loop fusion | flops 21233664 | bytes 42467328 | tf_op jit(solution)/shard_map/stack | solution.py:81
  401.0 19.9 %fusion.34 = (bf16[1,3,3,3,4,384,128]{6,1,5,4,0,3,2:T(4,128)(2,1)}, bf16[1,3,3,3,4,384,128]{6,1,5,4,0,3,2:T(4,128)(2,1)}) fusion(bf16[2,3,3,3,4,384,128]{6,1,5,4,0,3,2:T(4,128)(2,1)} %pad_maximum_fusion), kind=kLoop, calls=%fused_computation.67 | loop fusion | bytes 42467328 | tf_op jit(solution)/shard_map/slice | solution.py:84
  420.9 12.1 %copy.32 = bf16[1,3,3,3,4,384,128]{6,5,4,3,2,1,0:T(8,128)(2,1)} copy(bf16[1,3,3,3,4,384,128]{6,1,5,4,0,3,2:T(4,128)(2,1)} %get-tuple-element.81) | data formatting | bytes 21233664 | tf_op jit(solution)/shard_map/slice | solution.py:83
  434.0 5.8 copy.33
  439.8 180.3 %while.10 = (s32[]{:T(128)}, bf16[3,2,384,128]{3,2,1,0:T(8,128)(2,1)S(1)}, pred[3,2,27]{2,1,0:T(4,128)(4,1)S(1)}, bf16[3,2,384,128]{3,2,1,0:T(8,128)(2,1)}, s32[...) while((s32[]{:T(128)}, ...), condition=%wide.region_3.4_spmd, body=%wide.region_0.3_spmd.sunk | while | flops 4164648448 | bytes 127962088 | solution.py:103
  439.9 7.7 %gather_fusion.1 = bf16[54,384,128]{2,1,0:T(8,128)(2,1)} fusion(bf16[108,384,128]{2,1,0:T(8,128)(2,1)} %get-tuple-element.154, s32[1024]{0:T(1024)S(1)} %pad_clamp_fusion.2), kind=kCustom, calls=%fused_computation.clone.1 | custom fusion | bytes 10617048 | tf_op jit(solution)/shard_map/while/body/eval_jaxpr/gather | solution.py:101
  447.7 14.8 %fusion.47 = (f32[2,384]{1,0:T(2,128)S(1)}, f32[2,384,10368]{2,1,0:T(8,128)}) fusion(pred[2,10368]{1,0:T(4,128)(4,1)S(1)} %bitcast.96, bf16[2,10368,128]{2,1,0:T(8,128)(2,1)} %bitcast.86, bf16[3,2,384,128]{3,2,1,0:T(8,128)(2,1)} %get-tuple-element.152, s32[]{:T(128)} %get-tuple-element.141), kind=kOutput, calls=%fused_computation.4.clone.1 | convolution fusion | flops 2062318848 | bytes 37379840 | tf_op jit(solution)/shard_map/while/body/eval_jaxpr/jxg,jog->jxo/dot_general | solution.py:26
  462.5 14.3 %fusion.48 = f32[2,384]{1,0:T(2,128)S(1)} fusion(f32[2,384,10368]{2,1,0:T(8,128)} %get-tuple-element.131, f32[2,384]{1,0:T(2,128)S(1)} %get-tuple-element.132, pred[2,10368]{1,0:T(4,128)(4,1)S(1)} %bitcast.97), kind=kLoop, calls=%fused_computation.5.clone.1 | loop fusion | flops 31849728 | bytes 31877376 | tf_op jit(solution)/shard_map/while/body/eval_jaxpr/reduce_sum | solution.py:33
  476.8 7.7 %gather_fusion = bf16[54,384,128]{2,1,0:T(8,128)(2,1)} fusion(bf16[108,384,128]{2,1,0:T(8,128)(2,1)} %get-tuple-element.155, s32[1024]{0:T(1024)S(1)} %pad_clamp_fusion.2), kind=kCustom, calls=%fused_computation.1.clone.1 | custom fusion | bytes 10617048 | tf_op jit(solution)/shard_map/while/body/eval_jaxpr/gather | solution.py:101
  484.5 15.4 %fusion.49 = bf16[3,2,384,128]{3,2,1,0:T(8,128)(2,1)S(1)} fusion(bf16[3,2,384,128]{3,2,1,0:T(8,128)(2,1)S(1)} %get-tuple-element.142, s32[]{:T(128)} %get-tuple-element.141, bf16[2,10368,128]{2,1,0:T(8,128)(2,1)} %bitcast.87, f32[2,384,10368]{2,1,0:T(8,128)} %get-tuple-element.131, f32[2,384]{1,0:T(2,128)S(1)} %get-tuple-element.132, ...), kind=kOutput, calls=%fused_computation.12.clone.1 | convolution fusion | flops 2070478848 | bytes 37403140 | tf_op jit(solution)/shard_map/while/body/eval_jaxpr/aop,ape->aoe/dot_general | solution.py:34
  500.0 7.7 %gather_fusion.1 = bf16[54,384,128]{2,1,0:T(8,128)(2,1)} fusion(bf16[108,384,128]{2,1,0:T(8,128)(2,1)} %get-tuple-element.154, s32[1024]{0:T(1024)S(1)} %pad_clamp_fusion.2), kind=kCustom, calls=%fused_computation.clone.1 | custom fusion | bytes 10617048 | tf_op jit(solution)/shard_map/while/body/eval_jaxpr/gather | solution.py:101
  507.8 14.8 %fusion.47 = (f32[2,384]{1,0:T(2,128)S(1)}, f32[2,384,10368]{2,1,0:T(8,128)}) fusion(pred[2,10368]{1,0:T(4,128)(4,1)S(1)} %bitcast.96, bf16[2,10368,128]{2,1,0:T(8,128)(2,1)} %bitcast.86, bf16[3,2,384,128]{3,2,1,0:T(8,128)(2,1)} %get-tuple-element.152, s32[]{:T(128)} %get-tuple-element.141), kind=kOutput, calls=%fused_computation.4.clone.1 | convolution fusion | flops 2062318848 | bytes 37379840 | tf_op jit(solution)/shard_map/while/body/eval_jaxpr/jxg,jog->jxo/dot_general | solution.py:26
  522.6 14.3 %fusion.48 = f32[2,384]{1,0:T(2,128)S(1)} fusion(f32[2,384,10368]{2,1,0:T(8,128)} %get-tuple-element.131, f32[2,384]{1,0:T(2,128)S(1)} %get-tuple-element.132, pred[2,10368]{1,0:T(4,128)(4,1)S(1)} %bitcast.97), kind=kLoop, calls=%fused_computation.5.clone.1 | loop fusion | flops 31849728 | bytes 31877376 | tf_op jit(solution)/shard_map/while/body/eval_jaxpr/reduce_sum | solution.py:33
  536.9 7.7 %gather_fusion = bf16[54,384,128]{2,1,0:T(8,128)(2,1)} fusion(bf16[108,384,128]{2,1,0:T(8,128)(2,1)} %get-tuple-element.155, s32[1024]{0:T(1024)S(1)} %pad_clamp_fusion.2), kind=kCustom, calls=%fused_computation.1.clone.1 | custom fusion | bytes 10617048 | tf_op jit(solution)/shard_map/while/body/eval_jaxpr/gather | solution.py:101
  544.6 15.4 %fusion.49 = bf16[3,2,384,128]{3,2,1,0:T(8,128)(2,1)S(1)} fusion(bf16[3,2,384,128]{3,2,1,0:T(8,128)(2,1)S(1)} %get-tuple-element.142, s32[]{:T(128)} %get-tuple-element.141, bf16[2,10368,128]{2,1,0:T(8,128)(2,1)} %bitcast.87, f32[2,384,10368]{2,1,0:T(8,128)} %get-tuple-element.131, f32[2,384]{1,0:T(2,128)S(1)} %get-tuple-element.132, ...), kind=kOutput, calls=%fused_computation.12.clone.1 | convolution fusion | flops 2070478848 | bytes 37403140 | tf_op jit(solution)/shard_map/while/body/eval_jaxpr/aop,ape->aoe/dot_general | solution.py:34
  560.1 7.7 %gather_fusion.1 = bf16[54,384,128]{2,1,0:T(8,128)(2,1)} fusion(bf16[108,384,128]{2,1,0:T(8,128)(2,1)} %get-tuple-element.154, s32[1024]{0:T(1024)S(1)} %pad_clamp_fusion.2), kind=kCustom, calls=%fused_computation.clone.1 | custom fusion | bytes 10617048 | tf_op jit(solution)/shard_map/while/body/eval_jaxpr/gather | solution.py:101
  567.9 14.8 %fusion.47 = (f32[2,384]{1,0:T(2,128)S(1)}, f32[2,384,10368]{2,1,0:T(8,128)}) fusion(pred[2,10368]{1,0:T(4,128)(4,1)S(1)} %bitcast.96, bf16[2,10368,128]{2,1,0:T(8,128)(2,1)} %bitcast.86, bf16[3,2,384,128]{3,2,1,0:T(8,128)(2,1)} %get-tuple-element.152, s32[]{:T(128)} %get-tuple-element.141), kind=kOutput, calls=%fused_computation.4.clone.1 | convolution fusion | flops 2062318848 | bytes 37379840 | tf_op jit(solution)/shard_map/while/body/eval_jaxpr/jxg,jog->jxo/dot_general | solution.py:26
  582.7 14.3 %fusion.48 = f32[2,384]{1,0:T(2,128)S(1)} fusion(f32[2,384,10368]{2,1,0:T(8,128)} %get-tuple-element.131, f32[2,384]{1,0:T(2,128)S(1)} %get-tuple-element.132, pred[2,10368]{1,0:T(4,128)(4,1)S(1)} %bitcast.97), kind=kLoop, calls=%fused_computation.5.clone.1 | loop fusion | flops 31849728 | bytes 31877376 | tf_op jit(solution)/shard_map/while/body/eval_jaxpr/reduce_sum | solution.py:33
  597.0 7.7 %gather_fusion = bf16[54,384,128]{2,1,0:T(8,128)(2,1)} fusion(bf16[108,384,128]{2,1,0:T(8,128)(2,1)} %get-tuple-element.155, s32[1024]{0:T(1024)S(1)} %pad_clamp_fusion.2), kind=kCustom, calls=%fused_computation.1.clone.1 | custom fusion | bytes 10617048 | tf_op jit(solution)/shard_map/while/body/eval_jaxpr/gather | solution.py:101
  604.7 15.4 %fusion.49 = bf16[3,2,384,128]{3,2,1,0:T(8,128)(2,1)S(1)} fusion(bf16[3,2,384,128]{3,2,1,0:T(8,128)(2,1)S(1)} %get-tuple-element.142, s32[]{:T(128)} %get-tuple-element.141, bf16[2,10368,128]{2,1,0:T(8,128)(2,1)} %bitcast.87, f32[2,384,10368]{2,1,0:T(8,128)} %get-tuple-element.131, f32[2,384]{1,0:T(2,128)S(1)} %get-tuple-element.132, ...), kind=kOutput, calls=%fused_computation.12.clone.1 | convolution fusion | flops 2070478848 | bytes 37403140 | tf_op jit(solution)/shard_map/while/body/eval_jaxpr/aop,ape->aoe/dot_general | solution.py:34
  621.2 11.9 %all_to_all.25 = bf16[4,192,384]{2,1,0:T(8,128)(2,1)S(1)} all-to-all(bf16[4,192,384]{2,1,0:T(8,128)(2,1)S(1)} %all_to_all.18), channel_id=1, replica_groups=mesh['seq'=64,'head'=4] {'head'}, dimensions={0} | all-to-all | bytes 1179648 | tf_op jit(solution)/shard_map/all_to_all | solution.py:107
  (57 shorter events, 39.1 us)
Async XLA Ops:
  26.5 1.2 copy-start.3
  29.5 28.0 %collective-permute-start.1 = (bf16[2,3,2,384,128]{4,3,2,1,0:T(8,128)(2,1)}, bf16[2,3,2,384,128]{4,3,2,1,0:T(8,128)(2,1)}, u32[]{:S(2)}, u32[]{:S(2)}) collective-permute-start(bf16[2,3,2,384,128]{4,3,2,1,0:T(8,128)(2,1)} %copy.22), channel_id=1, source_target_pairs={{32,0},{36,4},{40,8},{44,12},{48,16},{52,20},{56,24},{60,28},{64,3... | collective-permute-start | bytes 3538952 | tf_op jit(solution)/shard_map/ppermute | solution.py:13
  33.1 53.3 %collective-permute-start = (bf16[2,3,2,384,128]{4,3,2,1,0:T(8,128)(2,1)}, bf16[2,3,2,384,128]{4,3,2,1,0:T(8,128)(2,1)}, u32[]{:S(2)}, u32[]{:S(2)}) collective-permute-start(bf16[2,3,2,384,128]{4,3,2,1,0:T(8,128)(2,1)} %copy.22), channel_id=1, source_target_pairs={{0,32},{4,36},{8,40},{12,44},{16,48},{20,52},{24,56},{28,60},{32,6... | collective-permute-start | bytes 3538952 | tf_op jit(solution)/shard_map/ppermute | solution.py:13
  88.6 89.5 %copy-start.1 = (bf16[2,3,2,384,128]{4,1,3,2,0:T(4,128)(2,1)}, bf16[2,3,2,384,128]{4,1,3,2,0:T(4,128)(2,1)S(1)}, u32[]{:S(2)}) copy-start(bf16[2,3,2,384,128]{4,1,3,2,0:T(4,128)(2,1)S(1)} %copy.48) | copy-start | bytes 3538948
  94.2 82.4 %collective-permute-start.2 = (bf16[2,3,3,384,128]{4,3,2,1,0:T(8,128)(2,1)S(1)}, bf16[2,3,3,384,128]{4,3,2,1,0:T(8,128)(2,1)S(1)}, u32[]{:S(2)}, u32[]{:S(2)}) collective-permute-start(bf16[2,3,3,384,128]{4,3,2,1,0:T(8,128)(2,1)S(1)} %copy.26), channel_id=1, source_target_pairs={{0,16},{4,20},{8,24},{12,28},{16,0},{20,4},{24,8},{28,12},{32,48},... | collective-permute-start | bytes 5308424 | tf_op jit(solution)/shard_map/ppermute | solution.py:19
  178.1 1.5 copy-start.2
  189.0 14.6 %copy-start.5 = (s32[3,2,27]{2,1,0:T(2,128)S(1)}, s32[3,2,27]{2,1,0:T(2,128)}, u32[]{:S(2)}) copy-start(s32[3,2,27]{2,1,0:T(2,128)} %param.5) | copy-start | bytes 1948
  197.5 154.9 %collective-permute-start.4 = (bf16[2,3,3,4,384,128]{5,4,3,2,1,0:T(8,128)(2,1)}, bf16[2,3,3,4,384,128]{5,4,3,2,1,0:T(8,128)(2,1)}, u32[]{:S(2)}, u32[]{:S(2)}) collective-permute-start(bf16[2,3,3,4,384,128]{5,4,3,2,1,0:T(8,128)(2,1)} %copy.28), channel_id=1, source_target_pairs={{4,0},{8,4},{12,8},{16,12},{20,16},{24,20},{28,24},{32,28},{36,32}... | collective-permute-start | bytes 21233672 | tf_op jit(solution)/shard_map/ppermute | solution.py:13
  199.4 163.3 %collective-permute-start.3 = (bf16[2,3,3,4,384,128]{5,4,3,2,1,0:T(8,128)(2,1)}, bf16[2,3,3,4,384,128]{5,4,3,2,1,0:T(8,128)(2,1)}, u32[]{:S(2)}, u32[]{:S(2)}) collective-permute-start(bf16[2,3,3,4,384,128]{5,4,3,2,1,0:T(8,128)(2,1)} %copy.28), channel_id=1, source_target_pairs={{0,4},{4,8},{8,12},{12,16},{16,20},{20,24},{24,28},{28,32},{32,36}... | collective-permute-start | bytes 21233672 | tf_op jit(solution)/shard_map/ppermute | solution.py:13
  420.9 13.1 %copy-start = (bf16[1,3,3,3,4,384,128]{6,1,5,4,0,3,2:T(4,128)(2,1)S(1)}, bf16[1,3,3,3,4,384,128]{6,1,5,4,0,3,2:T(4,128)(2,1)}, u32[]{:S(2)}) copy-start(bf16[1,3,3,3,4,384,128]{6,1,5,4,0,3,2:T(4,128)(2,1)} %get-tuple-element.80) | copy-start | bytes 31850500
  434.0 5.8 copy-start.4
